TPU v7x, 128 devices: a whole 4x4x4 slice. The times are simulated.
128 devices in a mesh: row: 16 (over x, z), col: 8 (over y, core).
Axes of the slice: x: 4, y: 4, z: 4, core: 2. Of those that a mesh axis runs over, the one named last changes fastest.
Arguments:
- block_values: bfloat16 [16, 8, 256, 128, 128], P('row', 'col')
- block_rows: int32 [16, 8, 256], P('row', 'col'), may hold values from -1 to 511, as said below
- block_cols: int32 [16, 8, 256], P('row', 'col'), may hold values from -1 to 511, as said below
- cost_vec: float32 [524288], P('col')
- demand: float32 [1048576], P('row')
- lower: float32 [524288], P('col'), may hold values from -1.5 to -0.2
- upper: float32 [524288], P('col'), may hold values from 0.2 to 1.5
- bound_kind: int32 [524288], P('col'), may hold values from 0 to 3
- primal_start: float32 [524288], P('col'), may hold values from -4 to 4
- dual_start: float32 [1048576], P('row'), may hold values from 0 to 1.5
Outputs:
- primal_out: float32 [524288], P('col')
- dual_out: float32 [1048576], P('row')
Inputs may be any that keep to these rules, and one draw needn't show every extreme that they name: A slot's block_rows and block_cols are both -1 exactly when the slot is empty; the live slots of a device come first, a device has at least 64 of them, and in every draw some device has all 256 slots live and some device has empty slots; every block row and every block column of the whole matrix is named by some live slot; a block place may be named by several slots. `block_cols`: as for block_rows.
All inputs are finite; a program needn't handle non-finite values.
Results may differ from a plain program's by a relative error of at most 0.0073.
Values sent between devices are 32-bit elements; how exact they have to be, the bound alone decides.
A program may use at most 64 MiB of HBM per device.

v0:
```python
import jax
import jax.numpy as jnp
from jax import lax
from jax.sharding import PartitionSpec as P

RUIZ_PASSES = 2
ITERS = 2
SMALL_EPS = 1e-06
STEP_SCALE = 0.3


def pick_tiles(vector, slot_ids, tile_count):
    tile_width = vector.shape[0] // tile_count
    padded = jnp.concatenate(
        [vector.reshape(tile_count, tile_width), jnp.zeros((1, tile_width), vector.dtype)], axis=0
    )
    return padded[slot_ids]


def tile_peaks(block_terms, slot_ids, tile_count):
    tile_width = block_terms.shape[1]
    return (
        jnp.zeros((tile_count + 1, tile_width), jnp.float32)
        .at[slot_ids]
        .max(block_terms)[:tile_count]
        .reshape(-1)
    )


def tile_sums(block_terms, slot_ids, tile_count):
    tile_width = block_terms.shape[1]
    return (
        jnp.zeros((tile_count + 1, tile_width), jnp.float32)
        .at[slot_ids]
        .add(block_terms)[:tile_count]
        .reshape(-1)
    )


def project_bounds(values, low_side, high_side, bound_types):
    lifted = jnp.where(
        (bound_types == 1) | (bound_types == 3), jnp.maximum(values, low_side), values
    )
    return jnp.where(
        (bound_types == 2) | (bound_types == 3), jnp.minimum(lifted, high_side), lifted
    )


def per_device(
    block_values,
    block_rows,
    block_cols,
    cost_vec,
    demand,
    lower,
    upper,
    bound_kind,
    primal_start,
    dual_start,
):
    values = block_values[0, 0]
    row_ids = block_rows[0, 0]
    col_ids = block_cols[0, 0]
    tile_width = values.shape[1]
    row_length = demand.shape[0]
    col_length = cost_vec.shape[0]
    row_count = row_length // tile_width
    col_count = col_length // tile_width
    live_slot = row_ids >= 0
    row_slot = jnp.where(live_slot, row_ids, row_count)
    col_slot = jnp.where(live_slot, col_ids, col_count)
    row_scale = jnp.ones((row_length,), jnp.float32)
    col_scale = jnp.ones((col_length,), jnp.float32)
    for pass_index in range(RUIZ_PASSES):
        row_part = pick_tiles(row_scale, row_slot, row_count)
        col_part = pick_tiles(col_scale, col_slot, col_count)
        scaled = jnp.abs(values).astype(jnp.float32) * row_part[:, :, None] * col_part[:, None, :]
        row_peak = lax.pmax(tile_peaks(jnp.max(scaled, axis=2), row_slot, row_count), "col")
        col_peak = lax.pmax(tile_peaks(jnp.max(scaled, axis=1), col_slot, col_count), "row")
        row_scale = row_scale / jnp.sqrt(row_peak + SMALL_EPS)
        col_scale = col_scale / jnp.sqrt(col_peak + SMALL_EPS)
    scaled_cost = col_scale * cost_vec
    scaled_demand = row_scale * demand
    cost_square = jnp.sum(scaled_cost * scaled_cost)
    demand_square = jnp.sum(scaled_demand * scaled_demand)
    cost_total = lax.psum(cost_square, "col")
    demand_total = lax.psum(demand_square, "row")
    norm_ratio = jnp.sqrt(cost_total + SMALL_EPS) / jnp.sqrt(demand_total + SMALL_EPS)
    primal_step = STEP_SCALE / norm_ratio
    dual_step = STEP_SCALE * norm_ratio
    primal = primal_start / col_scale
    dual_now = dual_start / row_scale
    low_side = lower / col_scale
    high_side = upper / col_scale
    for pass_index in range(ITERS):
        weights = (row_scale * dual_now).astype(jnp.bfloat16)
        picked = pick_tiles(weights, row_slot, row_count)
        partial_value = tile_sums(
            jnp.einsum("kij,ki->kj", values, picked, preferred_element_type=jnp.float32),
            col_slot,
            col_count,
        )
        gradient = col_scale * lax.psum(partial_value, "row")
        primal_next = project_bounds(
            primal - primal_step * (scaled_cost - gradient), low_side, high_side, bound_kind
        )
        shifted = (col_scale * (2.0 * primal_next - primal)).astype(jnp.bfloat16)
        picked = pick_tiles(shifted, col_slot, col_count)
        partial_value = tile_sums(
            jnp.einsum("kij,kj->ki", values, picked, preferred_element_type=jnp.float32),
            row_slot,
            row_count,
        )
        row_image = row_scale * lax.psum(partial_value, "col")
        dual_now = jnp.maximum(dual_now + dual_step * (scaled_demand - row_image), 0.0)
        primal = primal_next
    return (col_scale * primal, row_scale * dual_now)


def solution(mesh):
    return jax.shard_map(
        per_device,
        mesh=mesh,
        in_specs=(
            P("row", "col", None, None, None),
            P("row", "col", None),
            P("row", "col", None),
            P("col"),
            P("row"),
            P("col"),
            P("col"),
            P("col"),
            P("col"),
            P("row"),
        ),
        out_specs=(P("col"), P("row")),
        check_vma=False,
    )
```

profile of v0, /device:TPU:0, one launch (start us, length us, event | category | flops | bytes accessed | tf_op | source)
XLA Modules:
  0.0 671.1 jit_solution(2063073004390619092)
XLA Ops:
  7.2 0.0 all-reduce.18.cloned.1.call-start
  7.2 0.7 compare_select_fusion
  8.0 0.1 concatenate.25
  8.1 0.7 gather_fusion.1
  8.8 0.7 gather_fusion
  9.6 12.0 %fusion.1 = (f32[256,128]{1,0:T(8,128)S(1)}, f32[256,128]{1,0:T(8,128)S(1)}) fusion(f32[256,128]{1,0:T(8,128)S(1)} %gather_fusion.1, f32[256,128]{1,0:T(8,128)S(1)} %gather_fusion, bf16[1,1,256,128,128]{4,3,2,1,0:T(8,128)(2,1)} %param.10), kind=kLoop, calls=%fused_computation.19 | loop fusion | flops 25100288 | bytes 8912896 | tf_op jit(solution)/shard_map/reduce_max | solution.py:78
  21.5 1.7 scatter_custom_fusion.1
  23.2 0.7 slice_bitcast_fusion.6
  23.9 0.0 all-reduce.18.cloned.1.call-update
  24.0 0.0 all-reduce.16.cloned.1.call-start
  24.0 1.7 scatter_custom_fusion
  25.7 0.7 slice_bitcast_fusion.7
  26.4 0.0 all-reduce.16.cloned.1.call-update
  26.4 0.0 all-reduce.22.cloned.1.call-start
  26.5 60.2 %all-reduce.18.cloned.1.call-done = f32[65536]{0:T(1024)} async-done(((f32[65536]{0:T(1024)}), f32[65536]{0:T(1024)}) %all-reduce.18.cloned.1.call-update) | async-done | bytes 262160 | tf_op jit(solution)/shard_map/pmax | solution.py:78
  86.7 1.1 fusion.16
  87.8 0.7 gather_fusion.2
  88.6 85.9 %all-reduce.16.cloned.1.call-done = f32[65536]{0:T(1024)} async-done(((f32[65536]{0:T(1024)}), f32[65536]{0:T(1024)}) %all-reduce.16.cloned.1.call-update) | async-done | bytes 262160 | tf_op jit(solution)/shard_map/pmax | solution.py:79
  174.5 1.0 fusion.15
  175.5 0.7 gather_fusion.3
  176.2 11.9 %fusion.4 = (f32[256,128]{1,0:T(8,128)S(1)}, f32[256,128]{1,0:T(8,128)S(1)}) fusion(f32[256,128]{1,0:T(8,128)S(1)} %gather_fusion.3, f32[256,128]{1,0:T(8,128)S(1)} %gather_fusion.2, bf16[1,1,256,128,128]{4,3,2,1,0:T(8,128)(2,1)} %param.10), kind=kLoop, calls=%fused_computation.22 | loop fusion | flops 25100288 | bytes 8912896 | tf_op jit(solution)/shard_map/reduce_max | solution.py:78
  188.2 1.7 scatter_custom_fusion.3
  189.8 0.7 slice_bitcast_fusion.4
  190.6 0.0 all-reduce.22.cloned.1.call-update
  190.6 0.0 all-reduce.20.cloned.1.call-start
  190.6 1.7 scatter_custom_fusion.2
  192.3 0.7 slice_bitcast_fusion.5
  193.0 0.0 all-reduce.20.cloned.1.call-update
  193.1 0.0 all-reduce.24.cloned.1.call-start
  193.1 56.8 %all-reduce.22.cloned.1.call-done = f32[65536]{0:T(1024)} async-done(((f32[65536]{0:T(1024)}), f32[65536]{0:T(1024)}) %all-reduce.22.cloned.1.call-update) | async-done | bytes 262160 | tf_op jit(solution)/shard_map/pmax | solution.py:78
  249.9 1.7 multiply_reduce_fusion
  251.7 0.9 gather_fusion.4
  252.6 5.6 fusion.12
  258.2 1.7 scatter_custom_fusion.4
  259.9 0.7 slice_bitcast_fusion.3
  260.6 0.0 all-reduce.24.cloned.1.call-update
  260.7 0.0 all-reduce.26.cloned.1.call-start
  260.7 40.9 %psum.43 = f32[]{:T(128)} all-reduce(f32[]{:T(128)} %get-tuple-element.12), channel_id=1, replica_groups=mesh['row'=16,'col'=8] {'row'}, use_global_device_ids=true, to_apply=%region_15.16 | all-reduce | flops 1 | bytes 8 | tf_op jit(solution)/shard_map/psum | solution.py:87
  302.3 35.2 %all-reduce.20.cloned.1.call-done = f32[65536]{0:T(1024)} async-done(((f32[65536]{0:T(1024)}), f32[65536]{0:T(1024)}) %all-reduce.20.cloned.1.call-update) | async-done | bytes 262160 | tf_op jit(solution)/shard_map/pmax | solution.py:79
  337.5 1.6 multiply_reduce_fusion.1
  339.2 14.1 %psum.42 = f32[]{:T(128)} all-reduce(f32[]{:T(128)} %get-tuple-element.15), channel_id=1, replica_groups=mesh['row'=16,'col'=8] {'col'}, use_global_device_ids=true, to_apply=%region_10.11 | all-reduce | flops 1 | bytes 8 | tf_op jit(solution)/shard_map/psum | solution.py:86
  354.0 70.8 %all-reduce.24.cloned.1.call-done = f32[65536]{0:T(1024)} async-done(((f32[65536]{0:T(1024)}), f32[65536]{0:T(1024)}) %all-reduce.24.cloned.1.call-update) | async-done | bytes 262160 | tf_op jit(solution)/shard_map/psum | solution.py:103
  424.8 1.2 fusion.39
  426.0 0.9 gather_fusion.5
  426.9 7.8 %fusion.10 = f32[256,1,128]{2,1,0:T(1,128)S(1)} fusion(bf16[1,1,256,128,128]{4,3,2,1,0:T(8,128)(2,1)} %param.10, bf16[256,128,1]{1,0,2:T(8,128)(2,1)S(1)} %bitcast.68), kind=kOutput, calls=%fused_computation.28 | convolution fusion | flops 8388608 | bytes 8585216 | tf_op jit(solution)/shard_map/kij,kj->ki/dot_general | solution.py:110
  434.6 1.7 scatter_custom_fusion.5
  436.4 0.7 slice_bitcast_fusion.2
  437.1 0.0 all-reduce.26.cloned.1.call-update
  437.1 0.0 all-reduce.28.cloned.1.call-start
  437.1 59.2 %all-reduce.26.cloned.1.call-done = f32[65536]{0:T(1024)} async-done(((f32[65536]{0:T(1024)}), f32[65536]{0:T(1024)}) %all-reduce.26.cloned.1.call-update) | async-done | bytes 262160 | tf_op jit(solution)/shard_map/psum | solution.py:114
  496.3 1.0 fusion.34
  497.4 0.9 gather_fusion.6
  498.2 5.7 fusion.8
  503.9 1.7 scatter_custom_fusion.6
  505.6 0.7 slice_bitcast_fusion.1
  506.3 0.0 all-reduce.30.cloned.1.call-start
  506.4 83.9 %all-reduce.28.cloned.1.call-done = f32[65536]{0:T(1024)} async-done(((f32[65536]{0:T(1024)}), f32[65536]{0:T(1024)}) %all-reduce.28.cloned.1.call-update) | async-done | bytes 262160 | tf_op jit(solution)/shard_map/psum | solution.py:103
  590.3 1.9 fusion.40
  592.2 0.9 gather_fusion.7
  593.0 7.8 %fusion.6 = f32[256,1,128]{2,1,0:T(1,128)S(1)} fusion(bf16[1,1,256,128,128]{4,3,2,1,0:T(8,128)(2,1)} %param.10, bf16[256,128,1]{1,0,2:T(8,128)(2,1)S(1)} %bitcast.66), kind=kOutput, calls=%fused_computation.24 | convolution fusion | flops 8388608 | bytes 8585216 | tf_op jit(solution)/shard_map/kij,kj->ki/dot_general | solution.py:110
  600.8 1.7 scatter_custom_fusion.7
  602.5 0.7 slice_bitcast_fusion
  603.3 59.2 %all-reduce.30.cloned.1.call-done = f32[65536]{0:T(1024)} async-done(((f32[65536]{0:T(1024)}), f32[65536]{0:T(1024)}) %all-reduce.30.cloned.1.call-update) | async-done | bytes 262160 | tf_op jit(solution)/shard_map/psum | solution.py:114
  662.5 1.8 maximum_multiply_fusion
  (35 shorter events, 0.2 us)
Async XLA Ops:
  7.2 79.6 %all-reduce.18.cloned.1.call-start = ((), (), s32[]{:S(2)}) async-start(), calls=%async_computation.1 | async-start | bytes 524288 | tf_op jit(solution)/shard_map/pmax | solution.py:78
  23.9 226.0 %copy-start.4 = (f32[65536]{0:T(1024)S(1)}, f32[65536]{0:T(1024)}, u32[]{:S(2)}) copy-start(f32[65536]{0:T(1024)} %param.14) | copy-start | bytes 786436
  24.0 150.5 %all-reduce.16.cloned.1.call-start = ((), (), s32[]{:S(2)}) async-start(), calls=%async_computation | async-start | bytes 524288 | tf_op jit(solution)/shard_map/pmax | solution.py:79
  26.4 225.2 %copy-start.5 = (f32[65536]{0:T(1024)S(1)}, f32[65536]{0:T(1024)}, u32[]{:S(2)}) copy-start(f32[65536]{0:T(1024)} %param.19) | copy-start | bytes 786436
  26.4 223.5 %all-reduce.22.cloned.1.call-start = ((), (), s32[]{:S(2)}) async-start(), calls=%async_computation.3 | async-start | bytes 524288 | tf_op jit(solution)/shard_map/pmax | solution.py:78
  86.7 163.2 %copy-start.2 = (f32[65536]{0:T(1024)S(1)}, f32[65536]{0:T(1024)}, u32[]{:S(2)}) copy-start(f32[65536]{0:T(1024)} %all-reduce.18.cloned.1.call-done) | copy-start | bytes 786436
  188.1 149.4 %copy-start.1 = (f32[65536]{0:T(1024)S(1)}, f32[65536]{0:T(1024)}, u32[]{:S(2)}) copy-start(f32[65536]{0:T(1024)} %all-reduce.16.cloned.1.call-done) | copy-start | bytes 786436
  188.1 149.4 %copy-start.6 = (f32[65536]{0:T(1024)S(1)}, f32[65536]{0:T(1024)}, u32[]{:S(2)}) copy-start(f32[65536]{0:T(1024)} %param.13) | copy-start | bytes 786436
  188.1 236.6 %copy-start.7 = (f32[65536]{0:T(1024)S(1)}, f32[65536]{0:T(1024)}, u32[]{:S(2)}) copy-start(f32[65536]{0:T(1024)} %param.18) | copy-start | bytes 786436
  188.1 236.6 %copy-start.8 = (f32[65536]{0:T(1024)S(1)}, f32[65536]{0:T(1024)}, u32[]{:S(2)}) copy-start(f32[65536]{0:T(1024)} %param.15) | copy-start | bytes 786436
  188.1 236.6 %copy-start.9 = (s32[65536]{0:T(1024)S(1)}, s32[65536]{0:T(1024)}, u32[]{:S(2)}) copy-start(s32[65536]{0:T(1024)} %param.17) | copy-start | bytes 786436
  188.2 236.6 %copy-start.10 = (f32[65536]{0:T(1024)S(1)}, f32[65536]{0:T(1024)}, u32[]{:S(2)}) copy-start(f32[65536]{0:T(1024)} %param.16) | copy-start | bytes 786436
  190.6 146.9 %all-reduce.20.cloned.1.call-start = ((), (), s32[]{:S(2)}) async-start(), calls=%async_computation.2 | async-start | bytes 524288 | tf_op jit(solution)/shard_map/pmax | solution.py:79
  193.1 231.7 %all-reduce.24.cloned.1.call-start = ((), (), s32[]{:S(2)}) async-start(), calls=%async_computation.4 | async-start | bytes 524288 | tf_op jit(solution)/shard_map/psum | solution.py:103
  260.7 235.7 %all-reduce.26.cloned.1.call-start = ((), (), s32[]{:S(2)}) async-start(), calls=%async_computation.5 | async-start | bytes 524288 | tf_op jit(solution)/shard_map/psum | solution.py:114
  434.6 155.7 %copy-start = (f32[65536]{0:T(1024)S(1)}, f32[65536]{0:T(1024)}, u32[]{:S(2)}) copy-start(f32[65536]{0:T(1024)} %all-reduce.24.cloned.1.call-done) | copy-start | bytes 786436
  437.1 153.2 %all-reduce.28.cloned.1.call-start = ((), (), s32[]{:S(2)}) async-start(), calls=%async_computation.6 | async-start | bytes 524288 | tf_op jit(solution)/shard_map/psum | solution.py:103
  503.9 158.6 %copy-start.3 = (f32[65536]{0:T(1024)S(1)}, f32[65536]{0:T(1024)}, u32[]{:S(2)}) copy-start(f32[65536]{0:T(1024)} %all-reduce.26.cloned.1.call-done) | copy-start | bytes 786436
  506.3 156.2 %all-reduce.30.cloned.1.call-start = ((), (), s32[]{:S(2)}) async-start(), calls=%async_computation.7 | async-start | bytes 524288 | tf_op jit(solution)/shard_map/psum | solution.py:114
Sparse Core Ops, SparseCore 0:
  24.1 62.5 all-reduce.17
  90.8 83.6 all-reduce.15
  190.7 59.1 all-reduce.21
  253.9 83.5 all-reduce.19
  341.1 83.6 all-reduce.23
  437.2 59.0 all-reduce.25
  506.4 83.8 all-reduce.27
  603.4 59.0 all-reduce.29
where the time goes:
time: 672 us; the launch traced here: 671 us
  waiting for transfers between devices  512 us (76%)
  blocking collectives  55 us (8%)
  other arithmetic  49.3 us (7%)
  matrix products  26.9 us (4%)
  between operations  15.8 us (2%)
  local copies, waits for them, and re-layouts  12.4 us (2%)
    psum x2, waiting for transfers between devices, per_device(): gradient = col_scale * lax.psum(partial_value, 'row')  155 us
    pmax x2, waiting for transfers between devices, per_device(): lax.pmax(tile_peaks(jnp.max(scaled, axis=1), col_slot, col_count), 'row')  121 us
    psum x2, waiting for transfers between devices, per_device(): row_image = row_scale * lax.psum(partial_value, 'col')  118 us
    pmax x2, waiting for transfers between devices, per_device(): lax.pmax(tile_peaks(jnp.max(scaled, axis=2), row_slot, row_count), 'col')  117 us
    psum x1, blocking collectives, per_device(): demand_total = lax.psum(demand_square, 'row')  40.9 us
    reduce_max x2, other arithmetic, per_device(): jnp.max(scaled, axis=2)  23.8 us
    dot_general x2, matrix products, per_device(): jnp.einsum('kij,kj->ki', values, picked, preferred_element_type=jnp.float32)  15.6 us
    psum x1, blocking collectives, per_device(): cost_total = lax.psum(cost_square, 'col')  14.1 us
  transfers between devices with their start and end apart: 8, of which 8 were waited for; matrix products, arithmetic and copies ran while one was open for 3% of the time, Pallas kernels for 0%

commit v1 on v0

--- a/solution.py
+++ b/solution.py
@@ -7,6 +7,7 @@
 ITERS = 2
 SMALL_EPS = 1e-06
 STEP_SCALE = 0.3
+do_digits_here = lambda vec: jnp.sum(lax.all_gather(vec, "col"), axis=0)
 
 
 def pick_tiles(vector, slot_ids, tile_count):
@@ -111,7 +112,7 @@
             row_slot,
             row_count,
         )
-        row_image = row_scale * lax.psum(partial_value, "col")
+        row_image = row_scale * do_digits_here(partial_value)
         dual_now = jnp.maximum(dual_now + dual_step * (scaled_demand - row_image), 0.0)
         primal = primal_next
     return (col_scale * primal, row_scale * dual_now)

time: 672 us -> 609 us (0.906)
  waiting for transfers between devices: 512 us -> 443 us
    psum x2 -> x0, waiting for transfers between devices: 118 us -> none  [per_device(): row_image = row_scale * lax.psum(partial_value, 'col')]
    all_gather x0 -> x2, waiting for transfers between devices: none -> 49.1 us  [do_digits_here = lambda vec: jnp.sum(lax.all_gather(vec, 'col'), axis=0)]
where the time goes in v1:
time: 609 us; the launch traced here: 607 us
  waiting for transfers between devices  443 us (73%)
  blocking collectives  54.9 us (9%)
  other arithmetic  53.7 us (9%)
  matrix products  26.8 us (4%)
  between operations  15.7 us (3%)
  local copies, waits for them, and re-layouts  12.4 us (2%)
    psum x2, waiting for transfers between devices, per_device(): gradient = col_scale * lax.psum(partial_value, 'row')  156 us
    pmax x2, waiting for transfers between devices, per_device(): lax.pmax(tile_peaks(jnp.max(scaled, axis=1), col_slot, col_count), 'row')  121 us
    pmax x2, waiting for transfers between devices, per_device(): lax.pmax(tile_peaks(jnp.max(scaled, axis=2), row_slot, row_count), 'col')  117 us
    all_gather x2, waiting for transfers between devices, do_digits_here = lambda vec: jnp.sum(lax.all_gather(vec, 'col'), axis=0)  49.1 us
    psum x1, blocking collectives, per_device(): demand_total = lax.psum(demand_square, 'row')  40.8 us
    reduce_max x2, other arithmetic, per_device(): jnp.max(scaled, axis=2)  23.9 us
    dot_general x2, matrix products, per_device(): jnp.einsum('kij,kj->ki', values, picked, preferred_element_type=jnp.float32)  15.6 us
    psum x1, blocking collectives, per_device(): cost_total = lax.psum(cost_square, 'col')  14.1 us
  transfers between devices with their start and end apart: 8, of which 8 were waited for; matrix products, arithmetic and copies ran while one was open for 3% of the time, Pallas kernels for 0%

profile of v1, /device:TPU:0, one launch (start us, length us, event | category | flops | bytes accessed | tf_op | source)
XLA Modules:
  0.0 607.1 jit_solution(8570681838619352709)
XLA Ops:
  7.2 0.0 all-reduce.16.cloned.1.call-start
  7.2 0.7 compare_select_fusion
  8.0 0.1 concatenate.25
  8.1 0.7 gather_fusion.1
  8.8 0.7 gather_fusion
  9.6 12.0 %fusion.1 = (f32[256,128]{1,0:T(8,128)S(1)}, f32[256,128]{1,0:T(8,128)S(1)}) fusion(f32[256,128]{1,0:T(8,128)S(1)} %gather_fusion.1, f32[256,128]{1,0:T(8,128)S(1)} %gather_fusion, bf16[1,1,256,128,128]{4,3,2,1,0:T(8,128)(2,1)} %param.10), kind=kLoop, calls=%fused_computation.19 | loop fusion | flops 25100288 | bytes 8912896 | tf_op jit(solution)/shard_map/reduce_max | solution.py:79
  21.5 1.7 scatter_custom_fusion.1
  23.2 0.7 slice_bitcast_fusion.4
  23.9 0.0 all-reduce.16.cloned.1.call-update
  24.0 0.0 all-reduce.14.cloned.1.call-start
  24.0 1.7 scatter_custom_fusion
  25.7 0.7 slice_bitcast_fusion.5
  26.4 0.0 all-reduce.14.cloned.1.call-update
  26.4 0.0 all-reduce.20.cloned.1.call-start
  26.5 60.2 %all-reduce.16.cloned.1.call-done = f32[65536]{0:T(1024)} async-done(((f32[65536]{0:T(1024)}), f32[65536]{0:T(1024)}) %all-reduce.16.cloned.1.call-update) | async-done | bytes 262160 | tf_op jit(solution)/shard_map/pmax | solution.py:79
  86.7 1.1 fusion.16
  87.8 0.7 gather_fusion.2
  88.6 85.9 %all-reduce.14.cloned.1.call-done = f32[65536]{0:T(1024)} async-done(((f32[65536]{0:T(1024)}), f32[65536]{0:T(1024)}) %all-reduce.14.cloned.1.call-update) | async-done | bytes 262160 | tf_op jit(solution)/shard_map/pmax | solution.py:80
  174.5 1.0 fusion.15
  175.5 0.7 gather_fusion.3
  176.2 11.9 %fusion.4 = (f32[256,128]{1,0:T(8,128)S(1)}, f32[256,128]{1,0:T(8,128)S(1)}) fusion(f32[256,128]{1,0:T(8,128)S(1)} %gather_fusion.3, f32[256,128]{1,0:T(8,128)S(1)} %gather_fusion.2, bf16[1,1,256,128,128]{4,3,2,1,0:T(8,128)(2,1)} %param.10), kind=kLoop, calls=%fused_computation.22 | loop fusion | flops 25100288 | bytes 8912896 | tf_op jit(solution)/shard_map/reduce_max | solution.py:79
  188.2 1.7 scatter_custom_fusion.3
  189.9 0.7 slice_bitcast_fusion.2
  190.6 0.0 all-reduce.20.cloned.1.call-update
  190.6 0.0 all-reduce.18.cloned.1.call-start
  190.7 1.7 scatter_custom_fusion.2
  192.4 0.7 slice_bitcast_fusion.3
  193.1 0.0 all-reduce.18.cloned.1.call-update
  193.1 0.0 all-reduce.22.cloned.1.call-start
  193.2 56.8 %all-reduce.20.cloned.1.call-done = f32[65536]{0:T(1024)} async-done(((f32[65536]{0:T(1024)}), f32[65536]{0:T(1024)}) %all-reduce.20.cloned.1.call-update) | async-done | bytes 262160 | tf_op jit(solution)/shard_map/pmax | solution.py:79
  250.0 1.7 multiply_reduce_fusion
  251.8 0.9 gather_fusion.4
  252.6 5.6 fusion.12
  258.3 1.7 scatter_custom_fusion.4
  260.0 0.7 slice_bitcast_fusion.1
  260.7 0.0 all-gather.5.cloned.1.call-start
  260.8 40.8 %psum.29 = f32[]{:T(128)} all-reduce(f32[]{:T(128)} %get-tuple-element.12), channel_id=1, replica_groups=mesh['row'=16,'col'=8] {'row'}, use_global_device_ids=true, to_apply=%region_15.16 | all-reduce | flops 1 | bytes 8 | tf_op jit(solution)/shard_map/psum | solution.py:88
  302.2 35.4 %all-reduce.18.cloned.1.call-done = f32[65536]{0:T(1024)} async-done(((f32[65536]{0:T(1024)}), f32[65536]{0:T(1024)}) %all-reduce.18.cloned.1.call-update) | async-done | bytes 262160 | tf_op jit(solution)/shard_map/pmax | solution.py:80
  337.6 1.6 multiply_reduce_fusion.1
  339.2 14.1 %psum.28 = f32[]{:T(128)} all-reduce(f32[]{:T(128)} %get-tuple-element.15), channel_id=1, replica_groups=mesh['row'=16,'col'=8] {'col'}, use_global_device_ids=true, to_apply=%region_10.11 | all-reduce | flops 1 | bytes 8 | tf_op jit(solution)/shard_map/psum | solution.py:87
  354.1 70.8 %all-reduce.22.cloned.1.call-done = f32[65536]{0:T(1024)} async-done(((f32[65536]{0:T(1024)}), f32[65536]{0:T(1024)}) %all-reduce.22.cloned.1.call-update) | async-done | bytes 262160 | tf_op jit(solution)/shard_map/psum | solution.py:104
  424.9 1.2 fusion.39
  426.1 0.9 gather_fusion.5
  426.9 7.8 %fusion.10 = f32[256,1,128]{2,1,0:T(1,128)S(1)} fusion(bf16[1,1,256,128,128]{4,3,2,1,0:T(8,128)(2,1)} %param.10, bf16[256,128,1]{1,0,2:T(8,128)(2,1)S(1)} %bitcast.68), kind=kOutput, calls=%fused_computation.28 | convolution fusion | flops 8388608 | bytes 8585216 | tf_op jit(solution)/shard_map/kij,kj->ki/dot_general | solution.py:111
  434.7 1.7 scatter_custom_fusion.5
  436.4 0.7 slice.53
  437.2 0.0 all-reduce.24.cloned.1.call-start
  437.2 24.5 %all-gather.5.cloned.1.call-done = f32[8,1,65536]{2,1,0:T(1,128)} async-done(((f32[1,1,65536]{2,1,0:T(1,128)}), f32[8,1,65536]{2,1,0:T(1,128)}) %all-gather.5.cloned.1.call-update) | async-done | bytes 2097168 | tf_op jit(solution)/shard_map/all_gather | solution.py:10
  461.8 3.1 reduce_sum.38
  464.9 0.1 fusion.34
  465.0 0.9 gather_fusion.6
  465.8 5.6 fusion.8
  471.5 1.7 scatter_custom_fusion.6
  473.2 0.7 slice_bitcast_fusion
  473.9 0.0 all-gather.7.cloned.1.call-start
  474.0 84.8 %all-reduce.24.cloned.1.call-done = f32[65536]{0:T(1024)} async-done(((f32[65536]{0:T(1024)}), f32[65536]{0:T(1024)}) %all-reduce.24.cloned.1.call-update) | async-done | bytes 262160 | tf_op jit(solution)/shard_map/psum | solution.py:104
  558.8 1.9 fusion.40
  560.6 0.9 gather_fusion.7
  561.5 7.8 %fusion.6 = f32[256,1,128]{2,1,0:T(1,128)S(1)} fusion(bf16[1,1,256,128,128]{4,3,2,1,0:T(8,128)(2,1)} %param.10, bf16[256,128,1]{1,0,2:T(8,128)(2,1)S(1)} %bitcast.66), kind=kOutput, calls=%fused_computation.24 | convolution fusion | flops 8388608 | bytes 8585216 | tf_op jit(solution)/shard_map/kij,kj->ki/dot_general | solution.py:111
  569.3 1.7 scatter_custom_fusion.7
  571.0 0.7 slice.55
  571.7 24.6 %all-gather.7.cloned.1.call-done = f32[8,1,65536]{2,1,0:T(1,128)} async-done(((f32[1,1,65536]{2,1,0:T(1,128)}), f32[8,1,65536]{2,1,0:T(1,128)}) %all-gather.7.cloned.1.call-update) | async-done | bytes 2097168 | tf_op jit(solution)/shard_map/all_gather | solution.py:10
  596.3 3.1 reduce_sum.39
  599.4 0.8 maximum_multiply_fusion
  (35 shorter events, 0.3 us)
Async XLA Ops:
  7.2 79.6 %all-reduce.16.cloned.1.call-start = ((), (), s32[]{:S(2)}) async-start(), calls=%async_computation.1 | async-start | bytes 524288 | tf_op jit(solution)/shard_map/pmax | solution.py:79
  23.9 226.1 %copy-start.3 = (f32[65536]{0:T(1024)S(1)}, f32[65536]{0:T(1024)}, u32[]{:S(2)}) copy-start(f32[65536]{0:T(1024)} %param.14) | copy-start | bytes 786436
  24.0 150.5 %all-reduce.14.cloned.1.call-start = ((), (), s32[]{:S(2)}) async-start(), calls=%async_computation | async-start | bytes 524288 | tf_op jit(solution)/shard_map/pmax | solution.py:80
  26.4 225.3 %copy-start.4 = (f32[65536]{0:T(1024)S(1)}, f32[65536]{0:T(1024)}, u32[]{:S(2)}) copy-start(f32[65536]{0:T(1024)} %param.19) | copy-start | bytes 786436
  26.4 223.5 %all-reduce.20.cloned.1.call-start = ((), (), s32[]{:S(2)}) async-start(), calls=%async_computation.3 | async-start | bytes 524288 | tf_op jit(solution)/shard_map/pmax | solution.py:79
  86.7 163.3 %copy-start.2 = (f32[65536]{0:T(1024)S(1)}, f32[65536]{0:T(1024)}, u32[]{:S(2)}) copy-start(f32[65536]{0:T(1024)} %all-reduce.16.cloned.1.call-done) | copy-start | bytes 786436
  188.1 149.4 %copy-start.1 = (f32[65536]{0:T(1024)S(1)}, f32[65536]{0:T(1024)}, u32[]{:S(2)}) copy-start(f32[65536]{0:T(1024)} %all-reduce.14.cloned.1.call-done) | copy-start | bytes 786436
  188.2 149.4 %copy-start.5 = (f32[65536]{0:T(1024)S(1)}, f32[65536]{0:T(1024)}, u32[]{:S(2)}) copy-start(f32[65536]{0:T(1024)} %param.13) | copy-start | bytes 786436
  188.2 236.7 %copy-start.6 = (f32[65536]{0:T(1024)S(1)}, f32[65536]{0:T(1024)}, u32[]{:S(2)}) copy-start(f32[65536]{0:T(1024)} %param.18) | copy-start | bytes 786436
  188.2 236.7 %copy-start.7 = (f32[65536]{0:T(1024)S(1)}, f32[65536]{0:T(1024)}, u32[]{:S(2)}) copy-start(f32[65536]{0:T(1024)} %param.15) | copy-start | bytes 786436
  188.2 236.7 %copy-start.8 = (s32[65536]{0:T(1024)S(1)}, s32[65536]{0:T(1024)}, u32[]{:S(2)}) copy-start(s32[65536]{0:T(1024)} %param.17) | copy-start | bytes 786436
  188.2 236.6 %copy-start.9 = (f32[65536]{0:T(1024)S(1)}, f32[65536]{0:T(1024)}, u32[]{:S(2)}) copy-start(f32[65536]{0:T(1024)} %param.16) | copy-start | bytes 786436
  190.6 147.0 %all-reduce.18.cloned.1.call-start = ((), (), s32[]{:S(2)}) async-start(), calls=%async_computation.2 | async-start | bytes 524288 | tf_op jit(solution)/shard_map/pmax | solution.py:80
  193.1 231.7 %all-reduce.22.cloned.1.call-start = ((), (), s32[]{:S(2)}) async-start(), calls=%async_computation.4 | async-start | bytes 524288 | tf_op jit(solution)/shard_map/psum | solution.py:104
  260.7 201.1 %all-gather.5.cloned.1.call-start = ((), (), s32[]{:S(2)}) async-start(), calls=%async_computation.6 | async-start | bytes 2359296 | tf_op jit(solution)/shard_map/all_gather | solution.py:10
  434.7 124.0 %copy-start = (f32[65536]{0:T(1024)S(1)}, f32[65536]{0:T(1024)}, u32[]{:S(2)}) copy-start(f32[65536]{0:T(1024)} %all-reduce.22.cloned.1.call-done) | copy-start | bytes 786436
  437.2 121.6 %all-reduce.24.cloned.1.call-start = ((), (), s32[]{:S(2)}) async-start(), calls=%async_computation.5 | async-start | bytes 524288 | tf_op jit(solution)/shard_map/psum | solution.py:104
  473.9 122.4 %all-gather.7.cloned.1.call-start = ((), (), s32[]{:S(2)}) async-start(), calls=%async_computation.7 | async-start | bytes 2359296 | tf_op jit(solution)/shard_map/all_gather | solution.py:10
Sparse Core Ops, SparseCore 0:
  24.1 62.5 all-reduce.15
  90.8 83.6 all-reduce.13
  190.8 59.1 all-reduce.19
  253.9 83.6 all-reduce.17
  341.2 83.6 all-reduce.21
  437.3 24.4 all-gather.4
  474.0 84.6 all-reduce.23
  571.8 24.4 all-gather.6
